TPU v7x, 256 devices: a whole 4x4x8 slice. The times are simulated.
256 devices in a mesh: dp: 32 (over x, z), expert: 8 (over y, core).
Axes of the slice: x: 4, y: 4, z: 8, core: 2. Of those that a mesh axis runs over, the one named last changes fastest.
Arguments:
- tokens: bfloat16 [32768, 2048], P(('dp', 'expert')), may hold values from -24 to 24
- expert_ids: int32 [32768, 4], P(('dp', 'expert')), may hold values from 0 to 7, all different within a row; in each aligned block of 128 rows (0 to 127, 128 to 255, ...) at most 128 rows name the same one
- gates: bfloat16 [32768, 4], P(('dp', 'expert')), may hold values from 0.099609375 to 1
- w_gate: bfloat16 [8, 2048, 384], P('expert'), may hold values from -0.125 to 0.125
- w_up: bfloat16 [8, 2048, 384], P('expert'), may hold values from -0.125 to 0.125
- w_down: bfloat16 [8, 384, 2048], P('expert'), may hold values from -0.3125 to 0.3125
- cotangent: bfloat16 [32768, 2048], P(('dp', 'expert')), may hold values from -6 to 6
Outputs:
- mixed: bfloat16 [32768, 2048], P(('dp', 'expert'))
- grad_tokens: bfloat16 [32768, 2048], P(('dp', 'expert'))
- grad_gate: float32 [8, 2048, 384], P('expert', 'dp')
- grad_up: float32 [8, 2048, 384], P('expert', 'dp')
- grad_down: float32 [8, 384, 2048], P('expert', 'dp')
Inputs may be any that keep to these rules, and one draw needn't show every extreme that they name: `expert_ids`: each row names 4 different experts. In each aligned block of 128 rows (the rows of one device) no expert is named by more than 128 rows, a bound that some block reaches.
All inputs are finite; a program needn't handle non-finite values.
Results may differ from a plain program's by a relative error of at most 0.024.
Values may be sent and summed in bfloat16 or wider, within the bound.
A program may use at most 128 MiB of HBM per device.

v0:
```python
import jax
import jax.numpy as jnp
from jax import lax
from jax.sharding import PartitionSpec as P


def expert_rows(inputs, out_grads, gate_col, gate_panel, up_panel, down_panel):
    pre_gate = jnp.dot(inputs, gate_panel, preferred_element_type=jnp.float32)
    pre_up = jnp.dot(inputs, up_panel, preferred_element_type=jnp.float32)
    gate_sigmoid = jax.nn.sigmoid(pre_gate)
    activated = (pre_gate * gate_sigmoid * pre_up).astype(jnp.bfloat16)
    expert_out = jnp.dot(activated, down_panel, preferred_element_type=jnp.float32)
    contrib = (gate_col.astype(jnp.float32)[:, None] * expert_out).astype(jnp.bfloat16)
    act_grad = lax.dot_general(
        out_grads, down_panel, (((1,), (1,)), ((), ())), preferred_element_type=jnp.float32
    )
    up_grad = (act_grad * pre_gate * gate_sigmoid).astype(jnp.bfloat16)
    pre_grad = (act_grad * pre_up * gate_sigmoid * (1.0 + pre_gate * (1.0 - gate_sigmoid))).astype(
        jnp.bfloat16
    )
    grad_rows = lax.dot_general(
        pre_grad, gate_panel, (((1,), (1,)), ((), ())), preferred_element_type=jnp.float32
    )
    grad_rows = grad_rows + lax.dot_general(
        up_grad, up_panel, (((1,), (1,)), ((), ())), preferred_element_type=jnp.float32
    )
    grad_rows = grad_rows.astype(jnp.bfloat16)
    wgrad_gate = lax.dot_general(
        inputs, pre_grad, (((0,), (0,)), ((), ())), preferred_element_type=jnp.float32
    )
    wgrad_up = lax.dot_general(
        inputs, up_grad, (((0,), (0,)), ((), ())), preferred_element_type=jnp.float32
    )
    wgrad_down = lax.dot_general(
        activated, out_grads, (((0,), (0,)), ((), ())), preferred_element_type=jnp.float32
    )
    return (contrib, grad_rows, wgrad_gate, wgrad_up, wgrad_down)


def slot_table(route_ids, expert_num, per_source):
    token_count, pick_count = route_ids.shape
    matches = route_ids == expert_num
    hit_rows = jnp.any(matches, axis=1).astype(jnp.int32)
    which_pick = jnp.sum(
        matches.astype(jnp.int32) * jnp.arange(pick_count, dtype=jnp.int32)[None, :], axis=1
    )
    rank_of = jnp.cumsum(hit_rows) - hit_rows
    wanted = jnp.arange(per_source, dtype=jnp.int32)
    chosen = ((hit_rows[None, :] == 1) & (rank_of[None, :] == wanted[:, None])).astype(jnp.int32)
    valid_slot = jnp.sum(chosen, axis=1) > 0
    row_of = jnp.sum(chosen * jnp.arange(token_count, dtype=jnp.int32)[None, :], axis=1)
    pick_of = jnp.sum(chosen * which_pick[None, :], axis=1)
    return (row_of, pick_of, valid_slot)


def per_device(tokens, expert_ids, gates, w_gate, w_up, w_down, cotangent):
    tok_dev, model_width = tokens.shape
    group_size = lax.axis_size("expert")
    slot_count = group_size * tok_dev
    my_expert = lax.axis_index("expert")
    gate_panel = w_gate[0]
    up_panel = w_up[0]
    down_panel = w_down[0]
    all_rows, all_cot, all_gates = (
        lax.all_gather(tokens, "expert", axis=0, tiled=True),
        lax.all_gather(cotangent, "expert", axis=0, tiled=True),
        lax.all_gather(gates, "expert", axis=0, tiled=True),
    )
    all_ids = lax.all_gather(expert_ids, "expert", axis=0, tiled=True)
    source_ids = all_ids.reshape(group_size, tok_dev, all_ids.shape[1])
    row_of, pick_of, keep_mask = jax.vmap(
        lambda route_ids: slot_table(route_ids, my_expert, tok_dev)
    )(source_ids)
    flat_row = (row_of + jnp.arange(group_size, dtype=jnp.int32)[:, None] * tok_dev).reshape(
        slot_count
    )
    keep_b = keep_mask.reshape(slot_count).astype(jnp.bfloat16)
    inputs = all_rows[flat_row] * keep_b[:, None]
    gate_col = all_gates[flat_row, pick_of.reshape(slot_count)] * keep_b
    out_grads = (
        gate_col.astype(jnp.float32)[:, None] * all_cot[flat_row].astype(jnp.float32)
    ).astype(jnp.bfloat16)
    contrib, grad_rows, acc_gate, acc_up, acc_down = expert_rows(
        inputs, out_grads, gate_col, gate_panel, up_panel, down_panel
    )
    dest = jnp.where(keep_mask.reshape(slot_count), flat_row, group_size * tok_dev)
    part_out = (
        jnp.zeros((group_size * tok_dev, model_width), jnp.float32)
        .at[dest]
        .set(contrib.astype(jnp.float32), mode="drop")
    )
    part_grad = (
        jnp.zeros((group_size * tok_dev, model_width), jnp.float32)
        .at[dest]
        .set(grad_rows.astype(jnp.float32), mode="drop")
    )
    summed_out, summed_grad = (
        lax.psum_scatter(
            part_out.astype(jnp.bfloat16), "expert", scatter_dimension=0, tiled=True
        ).astype(jnp.float32),
        lax.psum_scatter(
            part_grad.astype(jnp.bfloat16), "expert", scatter_dimension=0, tiled=True
        ).astype(jnp.float32),
    )
    mixed = summed_out.astype(jnp.bfloat16)
    grad_tokens = summed_grad.astype(jnp.bfloat16)
    grad_gate, grad_up, grad_down = (
        lax.psum_scatter(
            acc_gate.astype(jnp.bfloat16), "dp", scatter_dimension=0, tiled=True
        ).astype(jnp.float32),
        lax.psum_scatter(acc_up.astype(jnp.bfloat16), "dp", scatter_dimension=0, tiled=True).astype(
            jnp.float32
        ),
        lax.psum_scatter(
            acc_down.astype(jnp.bfloat16), "dp", scatter_dimension=0, tiled=True
        ).astype(jnp.float32),
    )
    return (mixed, grad_tokens, grad_gate[None], grad_up[None], grad_down[None])


def solution(mesh):
    return jax.shard_map(
        per_device,
        mesh=mesh,
        in_specs=(
            P(("dp", "expert"), None),
            P(("dp", "expert"), None),
            P(("dp", "expert"), None),
            P("expert", None, None),
            P("expert", None, None),
            P("expert", None, None),
            P(("dp", "expert"), None),
        ),
        out_specs=(
            P(("dp", "expert"), None),
            P(("dp", "expert"), None),
            P("expert", "dp", None),
            P("expert", "dp", None),
            P("expert", "dp", None),
        ),
        check_vma=False,
    )
```

profile of v0, /device:TPU:2, one launch (start us, length us, event | category | flops | bytes accessed | tf_op | source)
XLA Modules:
  0.0 633.2 jit_solution(9545320917792145153)
XLA Ops:
  7.2 0.7 all-gather.3.cloned.1.call-update
  8.0 0.7 all-gather.5.cloned.1.call-update
  8.7 12.2 %all_gather.12 = s32[1024,4]{0,1:T(4,128)S(1)} all-gather(s32[128,4]{0,1:T(4,128)} %param.8), channel_id=1, replica_groups=mesh['dp'=32,'expert'=8] {'expert'}, dimensions={0}, use_global_device_ids=true | all-gather | bytes 18432 | tf_op jit(solution)/shard_map/all_gather | solution.py:69
  21.0 0.3 reduce_window_sum.11
  21.3 9.9 %all_gather.13 = bf16[1024,4]{0,1:T(4,128)(2,1)S(1)} all-gather(bf16[128,4]{0,1:T(4,128)(2,1)} %param.9), channel_id=1, replica_groups=mesh['dp'=32,'expert'=8] {'expert'}, dimensions={0}, use_global_device_ids=true | all-gather | bytes 9216 | tf_op jit(solution)/shard_map/all_gather | solution.py:67
  31.2 0.5 select_reduce_fusion
  31.7 0.1 broadcast_add_fusion
  31.8 9.1 %gather_fusion = bf16[1024]{0:T(1024)(128)(2,1)S(1)} fusion(bf16[1024,4]{0,1:T(4,128)(2,1)S(1)} %all_gather.13, s32[1024]{0:T(1024)S(1)} %bitcast.63), kind=kCustom, calls=%fused_computation | custom fusion | bytes 12288 | tf_op jit(solution)/shard_map/gather | solution.py:79
  40.9 6.6 %all-gather.3.cloned.1.call-done = bf16[1024,2048]{1,0:T(8,128)(2,1)} async-done(((bf16[128,2048]{1,0:T(8,128)(2,1)}), bf16[1024,2048]{1,0:T(8,128)(2,1)}) %all-gather.3.cloned.1.call-update) | async-done | bytes 4194320 | tf_op jit(solution)/shard_map/all_gather | solution.py:65
  47.6 11.5 %gather_fusion.1 = bf16[1024,2048]{1,0:T(8,128)(2,1)} fusion(bf16[1024,2048]{1,0:T(8,128)(2,1)} %all-gather.3.cloned.1.call-done, s32[1024]{0:T(1024)S(1)} %broadcast_clamp_fusion), kind=kCustom, calls=%fused_computation.1 | custom fusion | bytes 8392704 | tf_op jit(solution)/shard_map/gather | solution.py:78
  59.1 6.6 %fusion.9 = f32[1024,384]{1,0:T(8,128)} fusion(bf16[1024,2048]{1,0:T(8,128)(2,1)} %gather_fusion.1, bf16[1024]{0:T(1024)(128)(2,1)S(1)} %bitcast_convert_fusion.2, bf16[1,2048,384]{2,1,0:T(8,128)(2,1)} %param.11), kind=kOutput, calls=%fused_computation.19 | convolution fusion | flops 1612709888 | bytes 7342080 | tf_op jit(solution)/shard_map/dot_general | solution.py:9
  65.7 3.6 fusion.11
  69.3 14.8 %all-gather.5.cloned.1.call-done = bf16[1024,2048]{1,0:T(8,128)(2,1)} async-done(((bf16[128,2048]{1,0:T(8,128)(2,1)}), bf16[1024,2048]{1,0:T(8,128)(2,1)}) %all-gather.5.cloned.1.call-update) | async-done | bytes 4194320 | tf_op jit(solution)/shard_map/all_gather | solution.py:66
  84.1 11.5 %gather_fusion.2 = bf16[1024,2048]{1,0:T(8,128)(2,1)} fusion(bf16[1024,2048]{1,0:T(8,128)(2,1)} %all-gather.5.cloned.1.call-done, s32[1024]{0:T(1024)S(1)} %broadcast_clamp_fusion), kind=kCustom, calls=%fused_computation.2 | custom fusion | bytes 8392704 | tf_op jit(solution)/shard_map/gather | solution.py:81
  95.6 7.3 %multiply_convert_fusion.4 = (bf16[1024,384]{1,0:T(8,128)(2,1)S(1)}, bf16[1024,384]{1,0:T(8,128)(2,1)}, bf16[1024,384]{1,0:T(8,128)(2,1)}) fusion(f32[1024,384]{1,0:T(8,128)} %fusion.11, f32[1024,384]{1,0:T(8,128)} %fusion.9, bf16[1,384,2048]{2,1,0:T(8,128)(2,1)S(1)} %copy-done, bf16[1024,2048]{1,0:T(8,128)(2,1)} %gather_fusion.2, ...), kind=kOutput, calls=%fused_computation.35 | convolution fusion | flops 1623195648 | bytes 11276288 | tf_op jit(solution)/shard_map/dot_general | solution.py:14
  103.0 0.9 copy-done.5
  103.9 3.8 convolution_convert_fusion.1
  107.7 0.2 reduce-scatter.11.cloned.1.call-start
  107.9 6.1 convolution_convert_fusion.2
  114.1 5.4 multiply_convert_fusion.1
  119.5 10.9 %scatter_custom_fusion = f32[1024,2048]{1,0:T(8,128)} fusion(s32[1024]{0:T(1024)S(1)} %bitcast.70, bf16[1024,2048]{1,0:T(8,128)(2,1)} %multiply_convert_fusion.1, f32[]{:T(128)} %constant.10.clone.1), kind=kCustom, calls=%fused_computation.9 | custom fusion | flops 2097152 | bytes 12582916 | tf_op jit(solution)/shard_map/scatter | solution.py:90
  130.4 6.0 convert_element_type.93
  136.4 0.3 reduce-scatter.9.cloned.1.call-start
  136.7 3.6 fusion.22
  140.4 4.3 add_convert_fusion
  144.7 11.0 %scatter_custom_fusion.1 = f32[1024,2048]{1,0:T(8,128)} fusion(s32[1024]{0:T(1024)S(1)} %bitcast.71, bf16[1024,2048]{1,0:T(8,128)(2,1)} %add_convert_fusion, f32[]{:T(128)} %constant.10.clone.1), kind=kCustom, calls=%fused_computation.5 | custom fusion | flops 2097152 | bytes 12582916 | tf_op jit(solution)/shard_map/scatter | solution.py:95
  155.7 6.0 convert_element_type.100
  161.7 4.4 convolution_convert_fusion
  166.2 78.7 %fusion = bf16[16,2048]{1,0:T(8,128)(2,1)S(1)} fusion(bf16[384,2048]{1,0:T(8,128)(2,1)S(1)} %convolution_convert_fusion), kind=kCustom, calls=%all-reduce-scatter | all-reduce-scatter fusion | flops 1048577 | bytes 1639424
  244.9 2.5 collective-permute-start.6
  247.4 1.9 collective-permute-start.5
  249.4 10.2 %collective-permute-start.7 = (bf16[12,2048]{1,0:T(8,128)(2,1)S(1)}, bf16[12,2048]{1,0:T(8,128)(2,1)S(1)}, u32[]{:S(2)}, u32[]{:S(2)}) collective-permute-start(bf16[12,2048]{1,0:T(8,128)(2,1)S(1)} %slice.6), channel_id=1, source_target_pairs={{0,64},{8,72},{16,80},{24,88},{32,96},{40,104},{48,112},{56,120},{... | collective-permute-start | bytes 147464
  259.5 1.9 collective-permute-start.4
  261.4 9.1 %collective-permute-start.3 = (bf16[16,2048]{1,0:T(8,128)(2,1)S(1)}, bf16[16,2048]{1,0:T(8,128)(2,1)S(1)}, u32[]{:S(2)}, u32[]{:S(2)}) collective-permute-start(bf16[16,2048]{1,0:T(8,128)(2,1)S(1)} %fusion), channel_id=1, source_target_pairs={{0,32},{8,40},{16,48},{24,56},{32,64},{40,72},{48,80},{56,88},{64,... | collective-permute-start | bytes 196616
  270.6 1.9 collective-permute-start.2
  272.5 4.0 collective-permute-start.1
  276.5 3.4 collective-permute-start
  279.9 0.6 dynamic-slice.4
  281.2 2.2 collective-permute-done.1
  283.4 1.4 collective-permute-done
  284.8 1.4 concatenate.6
  286.3 0.7 copy.15
  287.0 36.3 %reduce-scatter.13.cloned.1.call-done = bf16[64,384]{1,0:T(8,128)(2,1)} async-done(((bf16[2048,384]{1,0:T(8,128)(2,1)}), bf16[64,384]{1,0:T(8,128)(2,1)}) %reduce-scatter.13.cloned.1.call-update) | async-done | bytes 49168 | tf_op jit(solution)/shard_map/reduce_scatter | solution.py:111
  323.3 1.4 bitcast_convert_fusion
  324.7 216.6 %reduce-scatter.11.cloned.1.call-done = bf16[64,384]{1,0:T(8,128)(2,1)} async-done(((bf16[2048,384]{1,0:T(8,128)(2,1)}), bf16[64,384]{1,0:T(8,128)(2,1)}) %reduce-scatter.11.cloned.1.call-update) | async-done | bytes 49168 | tf_op jit(solution)/shard_map/reduce_scatter | solution.py:108
  541.4 1.4 bitcast_convert_fusion.1
  542.8 41.2 %reduce-scatter.7.cloned.1.call-done = bf16[128,2048]{1,0:T(8,128)(2,1)} async-done(((bf16[1024,2048]{1,0:T(8,128)(2,1)}), bf16[128,2048]{1,0:T(8,128)(2,1)}) %reduce-scatter.7.cloned.1.call-update) | async-done | bytes 524304 | tf_op jit(solution)/shard_map/reduce_scatter | solution.py:98
  584.0 42.3 %reduce-scatter.9.cloned.1.call-done = bf16[128,2048]{1,0:T(8,128)(2,1)} async-done(((bf16[1024,2048]{1,0:T(8,128)(2,1)}), bf16[128,2048]{1,0:T(8,128)(2,1)}) %reduce-scatter.9.cloned.1.call-update) | async-done | bytes 524304 | tf_op jit(solution)/shard_map/reduce_scatter | solution.py:101
  (42 shorter events, 0.4 us)
Async XLA Ops:
  7.2 88.5 %copy-start = (bf16[1,384,2048]{2,1,0:T(8,128)(2,1)S(1)}, bf16[1,384,2048]{2,1,0:T(8,128)(2,1)}, u32[]{:S(2)}) copy-start(bf16[1,384,2048]{2,1,0:T(8,128)(2,1)} %param.12) | copy-start | bytes 4718596
  7.2 40.4 %all-gather.3.cloned.1.call-start = ((), (), s32[]{:S(2)}) async-start(), calls=%async_computation.4 | async-start | bytes 4718592 | tf_op jit(solution)/shard_map/all_gather | solution.py:65
  7.9 76.2 %all-gather.5.cloned.1.call-start = ((), (), s32[]{:S(2)}) async-start(), calls=%async_computation.6 | async-start | bytes 4718592 | tf_op jit(solution)/shard_map/all_gather | solution.py:66
  8.7 314.6 %reduce-scatter.13.cloned.1.call-start = ((), (), s32[]{:S(2)}) async-start(), calls=%async_computation.9 | async-start | bytes 1622016 | tf_op jit(solution)/shard_map/reduce_scatter | solution.py:111
  59.1 6.6 %copy-start.1 = (bf16[1024,2048]{1,0:T(8,128)(2,1)S(1)}, bf16[1024,2048]{1,0:T(8,128)(2,1)}, u32[]{:S(2)}) copy-start(bf16[1024,2048]{1,0:T(8,128)(2,1)} %gather_fusion.1) | copy-start | bytes 12582916
  59.1 6.6 %copy-start.3 = (bf16[1,2048,384]{2,1,0:T(8,128)(2,1)S(1)}, bf16[1,2048,384]{2,1,0:T(8,128)(2,1)}, u32[]{:S(2)}) copy-start(bf16[1,2048,384]{2,1,0:T(8,128)(2,1)} %param.10) | copy-start | bytes 4718596
  95.6 8.2 %copy-start.2 = (bf16[1024,2048]{1,0:T(8,128)(2,1)S(1)}, bf16[1024,2048]{1,0:T(8,128)(2,1)}, u32[]{:S(2)}) copy-start(bf16[1024,2048]{1,0:T(8,128)(2,1)} %gather_fusion.1) | copy-start | bytes 12582916
  103.0 0.9 copy-start.5
  107.7 433.7 %reduce-scatter.11.cloned.1.call-start = ((), (), s32[]{:S(2)}) async-start(), calls=%async_computation.8 | async-start | bytes 1622016 | tf_op jit(solution)/shard_map/reduce_scatter | solution.py:108
  114.0 470.0 %reduce-scatter.7.cloned.1.call-start = ((), (), s32[]{:S(2)}) async-start(), calls=%async_computation.5 | async-start | bytes 4718592 | tf_op jit(solution)/shard_map/reduce_scatter | solution.py:98
  136.4 489.9 %reduce-scatter.9.cloned.1.call-start = ((), (), s32[]{:S(2)}) async-start(), calls=%async_computation.7 | async-start | bytes 4718592 | tf_op jit(solution)/shard_map/reduce_scatter | solution.py:101
  136.7 3.7 copy-start.4
  136.7 3.7 copy-start.6
  161.7 118.2 %copy-start.7 = (u32[256]{0:T(256)S(1)}, u32[256]{0:T(256)}, u32[]{:S(2)}) copy-start(u32[256]{0:T(256)} %constant.53) | copy-start | bytes 3076
  244.9 27.6 %collective-permute-start.6 = (bf16[16,2048]{1,0:T(8,128)(2,1)S(1)}, bf16[16,2048]{1,0:T(8,128)(2,1)S(1)}, u32[]{:S(2)}, u32[]{:S(2)}) collective-permute-start(bf16[16,2048]{1,0:T(8,128)(2,1)S(1)} %fusion), channel_id=1, source_target_pairs={{0,56},{8,64},{16,72},{24,80},{32,88},{40,96},{48,104},{56,112},{6... | collective-permute-start | bytes 196616
  247.4 29.1 %collective-permute-start.5 = (bf16[16,2048]{1,0:T(8,128)(2,1)S(1)}, bf16[16,2048]{1,0:T(8,128)(2,1)S(1)}, u32[]{:S(2)}, u32[]{:S(2)}) collective-permute-start(bf16[16,2048]{1,0:T(8,128)(2,1)S(1)} %fusion), channel_id=1, source_target_pairs={{0,48},{8,56},{16,64},{24,72},{32,80},{40,88},{48,96},{56,104},{64... | collective-permute-start | bytes 196616
  249.4 21.2 %collective-permute-start.7 = (bf16[12,2048]{1,0:T(8,128)(2,1)S(1)}, bf16[12,2048]{1,0:T(8,128)(2,1)S(1)}, u32[]{:S(2)}, u32[]{:S(2)}) collective-permute-start(bf16[12,2048]{1,0:T(8,128)(2,1)S(1)} %slice.6), channel_id=1, source_target_pairs={{0,64},{8,72},{16,80},{24,88},{32,96},{40,104},{48,112},{56,120},{... | collective-permute-start | bytes 147464
  259.5 21.6 %collective-permute-start.4 = (bf16[16,2048]{1,0:T(8,128)(2,1)S(1)}, bf16[16,2048]{1,0:T(8,128)(2,1)S(1)}, u32[]{:S(2)}, u32[]{:S(2)}) collective-permute-start(bf16[16,2048]{1,0:T(8,128)(2,1)S(1)} %fusion), channel_id=1, source_target_pairs={{0,40},{8,48},{16,56},{24,64},{32,72},{40,80},{48,88},{56,96},{64,... | collective-permute-start | bytes 196616
  261.4 19.7 %collective-permute-start.3 = (bf16[16,2048]{1,0:T(8,128)(2,1)S(1)}, bf16[16,2048]{1,0:T(8,128)(2,1)S(1)}, u32[]{:S(2)}, u32[]{:S(2)}) collective-permute-start(bf16[16,2048]{1,0:T(8,128)(2,1)S(1)} %fusion), channel_id=1, source_target_pairs={{0,32},{8,40},{16,48},{24,56},{32,64},{40,72},{48,80},{56,88},{64,... | collective-permute-start | bytes 196616
  270.6 10.6 %collective-permute-start.2 = (bf16[16,2048]{1,0:T(8,128)(2,1)S(1)}, bf16[16,2048]{1,0:T(8,128)(2,1)S(1)}, u32[]{:S(2)}, u32[]{:S(2)}) collective-permute-start(bf16[16,2048]{1,0:T(8,128)(2,1)S(1)} %fusion), channel_id=1, source_target_pairs={{0,24},{8,32},{16,40},{24,48},{32,56},{40,64},{48,72},{56,80},{64,... | collective-permute-start | bytes 196616
  272.5 10.9 %collective-permute-start.1 = (bf16[16,2048]{1,0:T(8,128)(2,1)S(1)}, bf16[16,2048]{1,0:T(8,128)(2,1)S(1)}, u32[]{:S(2)}, u32[]{:S(2)}) collective-permute-start(bf16[16,2048]{1,0:T(8,128)(2,1)S(1)} %fusion), channel_id=1, source_target_pairs={{0,16},{8,24},{16,32},{24,40},{32,48},{40,56},{48,64},{56,72},{64,... | collective-permute-start | bytes 196616
  276.5 8.3 %collective-permute-start = (bf16[16,2048]{1,0:T(8,128)(2,1)S(1)}, bf16[16,2048]{1,0:T(8,128)(2,1)S(1)}, u32[]{:S(2)}, u32[]{:S(2)}) collective-permute-start(bf16[16,2048]{1,0:T(8,128)(2,1)S(1)} %fusion), channel_id=1, source_target_pairs={{0,8},{8,16},{16,24},{24,32},{32,40},{40,48},{48,56},{56,64},{64,7... | collective-permute-start | bytes 196616
Sparse Core Ops, SparseCore 0:
  9.9 37.6 all-gather.2
  49.4 34.6 all-gather.4
  107.8 215.4 reduce-scatter.12
  327.0 214.3 reduce-scatter.10
  544.4 39.5 reduce-scatter.6
  587.0 39.3 reduce-scatter.8
where the time goes:
time: 634 us; the launch traced here: 633 us
  waiting for transfers between devices  363 us (57%)
  blocking collectives  101 us (16%)
  matrix products  45.2 us (7%)
  other arithmetic  37.8 us (6%)
  local copies, waits for them, and re-layouts  35.9 us (6%)
  starting transfers between devices  35.5 us (6%)
  between operations  15.1 us (2%)
    reduce_scatter x1, waiting for transfers between devices, per_device(): lax.psum_scatter(acc_gate.astype(jnp.bfloat16), 'dp', scatter_dimension=0...  217 us
    unnamed x1, blocking collectives  78.7 us
    reduce_scatter x1, waiting for transfers between devices, per_device(): lax.psum_scatter(part_grad.astype(jnp.bfloat16), 'expert', scatter_dimens...  42.3 us
    reduce_scatter x1, waiting for transfers between devices, per_device(): lax.psum_scatter(part_out.astype(jnp.bfloat16), 'expert', scatter_dimensi...  41.2 us
    reduce_scatter x1, waiting for transfers between devices, per_device(): lax.psum_scatter(acc_up.astype(jnp.bfloat16), 'dp', scatter_dimension=0,...  36.3 us
    unnamed x8, starting transfers between devices  34.9 us
    all_gather x1, waiting for transfers between devices, per_device(): lax.all_gather(cotangent, 'expert', axis=0, tiled=True)  14.8 us
  transfers between devices with their start and end apart: 14, of which 8 were waited for; matrix products, arithmetic and copies ran while one was open for 27% of the time, Pallas kernels for 0%

commit v1 on v0

--- a/solution.py
+++ b/solution.py
@@ -54,6 +54,18 @@
 
 
 def per_device(tokens, expert_ids, gates, w_gate, w_up, w_down, cotangent):
+
+    def register_the_files(page):
+        return jnp.concatenate(
+            lax.all_to_all(
+                jnp.stack(lax.psum(1, axis_name="expert") * [page]),
+                axis_name="expert",
+                split_axis=0,
+                concat_axis=0,
+            ),
+            axis=0,
+        )
+
     tok_dev, model_width = tokens.shape
     group_size = lax.axis_size("expert")
     slot_count = group_size * tok_dev
@@ -63,7 +75,7 @@
     down_panel = w_down[0]
     all_rows, all_cot, all_gates = (
         lax.all_gather(tokens, "expert", axis=0, tiled=True),
-        lax.all_gather(cotangent, "expert", axis=0, tiled=True),
+        register_the_files(cotangent),
         lax.all_gather(gates, "expert", axis=0, tiled=True),
     )
     all_ids = lax.all_gather(expert_ids, "expert", axis=0, tiled=True)

time: 634 us -> 673 us (1.062)
  blocking collectives: 101 us -> 163 us
  waiting for transfers between devices: 363 us -> 339 us
    all_gather x1, blocking collectives: 12.2 us -> 71 us  [per_device(): all_ids = lax.all_gather(expert_ids, 'expert', axis=0, tiled=True)]
    all_gather x1 -> x0, waiting for transfers between devices: 14.8 us -> none  [per_device(): lax.all_gather(cotangent, 'expert', axis=0, tiled=True)]
  transfers between devices with their start and end apart: 14 -> 14, of which waited for: 8 -> 6; matrix products, arithmetic and copies ran while one was open for 27% -> 25% of each run, Pallas kernels for 0% -> 0%
where the time goes in v1:
time: 673 us; the launch traced here: 672 us
  waiting for transfers between devices  339 us (50%)
  blocking collectives  163 us (24%)
  local copies, waits for them, and re-layouts  39.4 us (6%)
  matrix products  39.3 us (6%)
  starting transfers between devices  39 us (6%)
  other arithmetic  37.8 us (6%)
  between operations  14.8 us (2%)
    reduce_scatter x1, waiting for transfers between devices, per_device(): lax.psum_scatter(acc_gate.astype(jnp.bfloat16), 'dp', scatter_dimension=0...  217 us
    unnamed x1, blocking collectives  82 us
    all_gather x1, blocking collectives, per_device(): all_ids = lax.all_gather(expert_ids, 'expert', axis=0, tiled=True)  71 us
    reduce_scatter x1, waiting for transfers between devices, per_device(): lax.psum_scatter(part_grad.astype(jnp.bfloat16), 'expert', scatter_dimens...  42.3 us
    reduce_scatter x1, waiting for transfers between devices, per_device(): lax.psum_scatter(part_out.astype(jnp.bfloat16), 'expert', scatter_dimensi...  41.1 us
    reduce_scatter x1, waiting for transfers between devices, per_device(): lax.psum_scatter(acc_up.astype(jnp.bfloat16), 'dp', scatter_dimension=0,...  34.8 us
    unnamed x8, starting transfers between devices  33.7 us
  transfers between devices with their start and end apart: 14, of which 6 were waited for; matrix products, arithmetic and copies ran while one was open for 25% of the time, Pallas kernels for 0%

profile of v1, /device:TPU:2, one launch (start us, length us, event | category | flops | bytes accessed | tf_op | source)
XLA Modules:
  0.0 672.5 jit_solution(13478985650277986934)
XLA Ops:
  7.2 0.7 all-gather.2.cloned.1.call-update
  7.9 3.5 stack.2
  11.4 4.7 all-to-all-start
  16.1 0.0 reduce-scatter.13.cloned.1.call-start
  16.2 71.0 %all_gather.9 = s32[1024,4]{0,1:T(4,128)S(1)} all-gather(s32[128,4]{0,1:T(4,128)S(1)} %copy-done.7), channel_id=1, replica_groups=mesh['dp'=32,'expert'=8] {'expert'}, dimensions={0}, use_global_device_ids=true | all-gather | bytes 18432 | tf_op jit(solution)/shard_map/all_gather | solution.py:81
  87.2 0.3 reduce_window_sum.11
  87.5 9.9 %all_gather.10 = bf16[1024,4]{0,1:T(4,128)(2,1)S(1)} all-gather(bf16[128,4]{0,1:T(4,128)(2,1)S(1)} %copy-done.8), channel_id=1, replica_groups=mesh['dp'=32,'expert'=8] {'expert'}, dimensions={0}, use_global_device_ids=true | all-gather | bytes 9216 | tf_op jit(solution)/shard_map/all_gather | solution.py:79
  97.5 0.5 select_reduce_fusion
  98.0 0.1 broadcast_add_fusion
  98.1 9.1 %gather_fusion = bf16[1024]{0:T(1024)(128)(2,1)S(1)} fusion(bf16[1024,4]{0,1:T(4,128)(2,1)S(1)} %all_gather.10, s32[1024]{0:T(1024)S(1)} %bitcast.64), kind=kCustom, calls=%fused_computation | custom fusion | bytes 12288 | tf_op jit(solution)/shard_map/gather | solution.py:91
  107.2 11.5 %gather_fusion.2 = bf16[1024,2048]{1,0:T(8,128)(2,1)} fusion(bf16[1024,2048]{1,0:T(8,128)(2,1)} %bitcast.11, s32[1024]{0:T(1024)S(1)} %broadcast_clamp_fusion), kind=kCustom, calls=%fused_computation.2 | custom fusion | bytes 8392704 | tf_op jit(solution)/shard_map/gather | solution.py:93
  118.7 11.5 %gather_fusion.1 = bf16[1024,2048]{1,0:T(8,128)(2,1)} fusion(bf16[1024,2048]{1,0:T(8,128)(2,1)} %all-gather.2.cloned.1.call-done, s32[1024]{0:T(1024)S(1)} %broadcast_clamp_fusion), kind=kCustom, calls=%fused_computation.1 | custom fusion | bytes 8392704 | tf_op jit(solution)/shard_map/gather | solution.py:90
  130.3 5.2 fusion.9
  135.5 2.4 fusion.11
  137.9 4.1 multiply_convert_fusion.4
  142.0 0.9 copy-done.5
  142.9 3.8 convolution_convert_fusion.1
  146.7 0.2 reduce-scatter.11.cloned.1.call-start
  146.9 6.1 convolution_convert_fusion.2
  153.1 5.4 multiply_convert_fusion.1
  158.5 10.9 %scatter_custom_fusion = f32[1024,2048]{1,0:T(8,128)} fusion(s32[1024]{0:T(1024)S(1)} %bitcast.71, bf16[1024,2048]{1,0:T(8,128)(2,1)} %multiply_convert_fusion.1, f32[]{:T(128)} %constant.10.clone.1), kind=kCustom, calls=%fused_computation.9 | custom fusion | flops 2097152 | bytes 12582916 | tf_op jit(solution)/shard_map/scatter | solution.py:102
  169.4 6.0 convert_element_type.93
  175.4 0.3 reduce-scatter.9.cloned.1.call-start
  175.7 3.7 fusion.22
  179.4 4.3 add_convert_fusion
  183.7 10.9 %scatter_custom_fusion.1 = f32[1024,2048]{1,0:T(8,128)} fusion(s32[1024]{0:T(1024)S(1)} %bitcast.72, bf16[1024,2048]{1,0:T(8,128)(2,1)} %add_convert_fusion, f32[]{:T(128)} %constant.10.clone.1), kind=kCustom, calls=%fused_computation.5 | custom fusion | flops 2097152 | bytes 12582916 | tf_op jit(solution)/shard_map/scatter | solution.py:107
  194.7 6.0 convert_element_type.100
  200.7 4.4 convolution_convert_fusion
  205.2 82.0 %fusion = bf16[16,2048]{1,0:T(8,128)(2,1)S(1)} fusion(bf16[384,2048]{1,0:T(8,128)(2,1)S(1)} %convolution_convert_fusion), kind=kCustom, calls=%all-reduce-scatter | all-reduce-scatter fusion | flops 1048577 | bytes 1639424
  287.2 1.9 collective-permute-start.6
  289.1 1.9 collective-permute-start.5
  291.1 9.5 %collective-permute-start.7 = (bf16[12,2048]{1,0:T(8,128)(2,1)S(1)}, bf16[12,2048]{1,0:T(8,128)(2,1)S(1)}, u32[]{:S(2)}, u32[]{:S(2)}) collective-permute-start(bf16[12,2048]{1,0:T(8,128)(2,1)S(1)} %slice.6), channel_id=1, source_target_pairs={{0,64},{8,72},{16,80},{24,88},{32,96},{40,104},{48,112},{56,120},{... | collective-permute-start | bytes 147464
  300.6 1.9 collective-permute-start.4
  302.5 9.1 %collective-permute-start.3 = (bf16[16,2048]{1,0:T(8,128)(2,1)S(1)}, bf16[16,2048]{1,0:T(8,128)(2,1)S(1)}, u32[]{:S(2)}, u32[]{:S(2)}) collective-permute-start(bf16[16,2048]{1,0:T(8,128)(2,1)S(1)} %fusion), channel_id=1, source_target_pairs={{0,32},{8,40},{16,48},{24,56},{32,64},{40,72},{48,80},{56,88},{64,... | collective-permute-start | bytes 196616
  311.7 1.9 collective-permute-start.2
  313.6 4.0 collective-permute-start.1
  317.6 3.4 collective-permute-start
  321.0 0.6 dynamic-slice.4
  322.3 2.2 collective-permute-done.1
  324.5 1.4 collective-permute-done
  325.9 1.4 concatenate.6
  327.4 0.7 copy.15
  328.1 34.8 %reduce-scatter.13.cloned.1.call-done = bf16[64,384]{1,0:T(8,128)(2,1)} async-done(((bf16[2048,384]{1,0:T(8,128)(2,1)}), bf16[64,384]{1,0:T(8,128)(2,1)}) %reduce-scatter.13.cloned.1.call-update) | async-done | bytes 49168 | tf_op jit(solution)/shard_map/reduce_scatter | solution.py:123
  362.9 1.4 bitcast_convert_fusion
  364.4 216.8 %reduce-scatter.11.cloned.1.call-done = bf16[64,384]{1,0:T(8,128)(2,1)} async-done(((bf16[2048,384]{1,0:T(8,128)(2,1)}), bf16[64,384]{1,0:T(8,128)(2,1)}) %reduce-scatter.11.cloned.1.call-update) | async-done | bytes 49168 | tf_op jit(solution)/shard_map/reduce_scatter | solution.py:120
  581.2 1.4 bitcast_convert_fusion.1
  582.6 41.1 %reduce-scatter.7.cloned.1.call-done = bf16[128,2048]{1,0:T(8,128)(2,1)} async-done(((bf16[1024,2048]{1,0:T(8,128)(2,1)}), bf16[128,2048]{1,0:T(8,128)(2,1)}) %reduce-scatter.7.cloned.1.call-update) | async-done | bytes 524304 | tf_op jit(solution)/shard_map/reduce_scatter | solution.py:110
  623.7 42.3 %reduce-scatter.9.cloned.1.call-done = bf16[128,2048]{1,0:T(8,128)(2,1)} async-done(((bf16[1024,2048]{1,0:T(8,128)(2,1)}), bf16[128,2048]{1,0:T(8,128)(2,1)}) %reduce-scatter.9.cloned.1.call-update) | async-done | bytes 524304 | tf_op jit(solution)/shard_map/reduce_scatter | solution.py:113
  (46 shorter events, 0.4 us)
Async XLA Ops:
  7.2 130.7 %copy-start = (bf16[1,384,2048]{2,1,0:T(8,128)(2,1)S(1)}, bf16[1,384,2048]{2,1,0:T(8,128)(2,1)}, u32[]{:S(2)}) copy-start(bf16[1,384,2048]{2,1,0:T(8,128)(2,1)} %param.12) | copy-start | bytes 4718596
  7.2 111.5 %all-gather.2.cloned.1.call-start = ((), (), s32[]{:S(2)}) async-start(), calls=%async_computation.5 | async-start | bytes 4718592 | tf_op jit(solution)/shard_map/all_gather | solution.py:77
  11.4 4.7 copy-start.7
  11.4 76.1 %copy-start.8 = (bf16[128,4]{0,1:T(4,128)(2,1)S(1)}, bf16[128,4]{0,1:T(4,128)(2,1)}, u32[]{:S(2)}) copy-start(bf16[128,4]{0,1:T(4,128)(2,1)} %param.9) | copy-start | bytes 3076
  11.4 95.7 %all-to-all-start = ((bf16[8,128,2048]{2,1,0:T(8,128)(2,1)}), bf16[8,128,2048]{2,1,0:T(8,128)(2,1)}, u32[]{:S(2)}, u32[]{:S(2)}) async-start(bf16[8,128,2048]{2,1,0:T(8,128)(2,1)} %stack.2), calls=%async_computation.1 | async-start | bytes 8388608 | tf_op jit(solution)/shard_map/all_to_all | solution.py:60
  16.1 346.8 %reduce-scatter.13.cloned.1.call-start = ((), (), s32[]{:S(2)}) async-start(), calls=%async_computation.9 | async-start | bytes 1622016 | tf_op jit(solution)/shard_map/reduce_scatter | solution.py:123
  130.2 5.2 copy-start.2
  130.2 5.2 copy-start.3
  135.5 2.4 copy-start.1
  142.0 0.9 copy-start.5
  146.7 434.5 %reduce-scatter.11.cloned.1.call-start = ((), (), s32[]{:S(2)}) async-start(), calls=%async_computation.8 | async-start | bytes 1622016 | tf_op jit(solution)/shard_map/reduce_scatter | solution.py:120
  153.0 470.7 %reduce-scatter.7.cloned.1.call-start = ((), (), s32[]{:S(2)}) async-start(), calls=%async_computation.6 | async-start | bytes 4718592 | tf_op jit(solution)/shard_map/reduce_scatter | solution.py:110
  175.4 490.5 %reduce-scatter.9.cloned.1.call-start = ((), (), s32[]{:S(2)}) async-start(), calls=%async_computation.7 | async-start | bytes 4718592 | tf_op jit(solution)/shard_map/reduce_scatter | solution.py:113
  175.7 3.7 copy-start.4
  175.7 3.7 copy-start.6
  200.7 120.3 %copy-start.9 = (u32[256]{0:T(256)S(1)}, u32[256]{0:T(256)}, u32[]{:S(2)}) copy-start(u32[256]{0:T(256)} %constant.53) | copy-start | bytes 3076
  287.2 26.4 %collective-permute-start.6 = (bf16[16,2048]{1,0:T(8,128)(2,1)S(1)}, bf16[16,2048]{1,0:T(8,128)(2,1)S(1)}, u32[]{:S(2)}, u32[]{:S(2)}) collective-permute-start(bf16[16,2048]{1,0:T(8,128)(2,1)S(1)} %fusion), channel_id=1, source_target_pairs={{0,56},{8,64},{16,72},{24,80},{32,88},{40,96},{48,104},{56,112},{6... | collective-permute-start | bytes 196616
  289.1 28.5 %collective-permute-start.5 = (bf16[16,2048]{1,0:T(8,128)(2,1)S(1)}, bf16[16,2048]{1,0:T(8,128)(2,1)S(1)}, u32[]{:S(2)}, u32[]{:S(2)}) collective-permute-start(bf16[16,2048]{1,0:T(8,128)(2,1)S(1)} %fusion), channel_id=1, source_target_pairs={{0,48},{8,56},{16,64},{24,72},{32,80},{40,88},{48,96},{56,104},{64... | collective-permute-start | bytes 196616
  291.1 20.6 %collective-permute-start.7 = (bf16[12,2048]{1,0:T(8,128)(2,1)S(1)}, bf16[12,2048]{1,0:T(8,128)(2,1)S(1)}, u32[]{:S(2)}, u32[]{:S(2)}) collective-permute-start(bf16[12,2048]{1,0:T(8,128)(2,1)S(1)} %slice.6), channel_id=1, source_target_pairs={{0,64},{8,72},{16,80},{24,88},{32,96},{40,104},{48,112},{56,120},{... | collective-permute-start | bytes 147464
  300.6 21.7 %collective-permute-start.4 = (bf16[16,2048]{1,0:T(8,128)(2,1)S(1)}, bf16[16,2048]{1,0:T(8,128)(2,1)S(1)}, u32[]{:S(2)}, u32[]{:S(2)}) collective-permute-start(bf16[16,2048]{1,0:T(8,128)(2,1)S(1)} %fusion), channel_id=1, source_target_pairs={{0,40},{8,48},{16,56},{24,64},{32,72},{40,80},{48,88},{56,96},{64,... | collective-permute-start | bytes 196616
  302.5 19.7 %collective-permute-start.3 = (bf16[16,2048]{1,0:T(8,128)(2,1)S(1)}, bf16[16,2048]{1,0:T(8,128)(2,1)S(1)}, u32[]{:S(2)}, u32[]{:S(2)}) collective-permute-start(bf16[16,2048]{1,0:T(8,128)(2,1)S(1)} %fusion), channel_id=1, source_target_pairs={{0,32},{8,40},{16,48},{24,56},{32,64},{40,72},{48,80},{56,88},{64,... | collective-permute-start | bytes 196616
  311.7 10.6 %collective-permute-start.2 = (bf16[16,2048]{1,0:T(8,128)(2,1)S(1)}, bf16[16,2048]{1,0:T(8,128)(2,1)S(1)}, u32[]{:S(2)}, u32[]{:S(2)}) collective-permute-start(bf16[16,2048]{1,0:T(8,128)(2,1)S(1)} %fusion), channel_id=1, source_target_pairs={{0,24},{8,32},{16,40},{24,48},{32,56},{40,64},{48,72},{56,80},{64,... | collective-permute-start | bytes 196616
  313.6 10.9 %collective-permute-start.1 = (bf16[16,2048]{1,0:T(8,128)(2,1)S(1)}, bf16[16,2048]{1,0:T(8,128)(2,1)S(1)}, u32[]{:S(2)}, u32[]{:S(2)}) collective-permute-start(bf16[16,2048]{1,0:T(8,128)(2,1)S(1)} %fusion), channel_id=1, source_target_pairs={{0,16},{8,24},{16,32},{24,40},{32,48},{40,56},{48,64},{56,72},{64,... | collective-permute-start | bytes 196616
  317.6 8.3 %collective-permute-start = (bf16[16,2048]{1,0:T(8,128)(2,1)S(1)}, bf16[16,2048]{1,0:T(8,128)(2,1)S(1)}, u32[]{:S(2)}, u32[]{:S(2)}) collective-permute-start(bf16[16,2048]{1,0:T(8,128)(2,1)S(1)} %fusion), channel_id=1, source_target_pairs={{0,8},{8,16},{16,24},{24,32},{32,40},{40,48},{48,56},{56,64},{64,7... | collective-permute-start | bytes 196616
Sparse Core Ops, SparseCore 0:
  9.9 59.3 all-gather.1
  146.8 216.0 reduce-scatter.12
  366.8 214.3 reduce-scatter.10
  584.1 39.4 reduce-scatter.6
  626.6 39.2 reduce-scatter.8
